TPU v7x, 32 devices: a whole 2x2x4 slice. The times are simulated.
32 devices in a mesh: grp: 2 (over y), seq: 4 (over z), head: 2 (over x), sub: 2 (over core).
Axes of the slice: x: 2, y: 2, z: 4, core: 2. Of those that a mesh axis runs over, the one named last changes fastest.
Arguments:
- queries: float32 [1536, 2048], P(('grp', 'seq'), ('head', 'sub')), parts along dimension 0, may hold values from -6 to 6
- keys: float32 [1536, 2048], P(('grp', 'seq'), ('head', 'sub')), parts along dimension 0, may hold values from -6 to 6
- values: float32 [1536, 2048], P(('grp', 'seq'), ('head', 'sub')), parts along dimension 0, may hold values from -40 to 40
- opt_queries: float32 [16, 64, 2048], P(('grp', 'seq'), None, ('head', 'sub')), parts along dimension 0, may hold values from -6 to 6
- opt_keys: float32 [16, 64, 2048], P(('grp', 'seq'), None, ('head', 'sub')), parts along dimension 0, may hold values from -6 to 6
- opt_values: float32 [16, 64, 2048], P(('grp', 'seq'), None, ('head', 'sub')), parts along dimension 0, may hold values from -40 to 40
- opt_offsets: int32 [16], P(('grp', 'seq')), parts along dimension 0, may hold values from 0 to 192
- opt_lengths: int32 [16], P(('grp', 'seq')), parts along dimension 0, may hold values from 1 to 64, 320 in all
- norm_gain: float32 [2048], P(('head', 'sub')), may hold values from 0.5 to 2
- out_weight: bfloat16 [2048, 4096], P(('head', 'sub')), may hold values from -0.125 to 0.125
Outputs:
- ctx_out: bfloat16 [1536, 4096], P(('grp', 'seq'), ('head', 'sub')), parts along dimension 0
- opt_out: bfloat16 [16, 64, 4096], P(('grp', 'seq'), None, ('head', 'sub')), parts along dimension 0
There are 2 independent parts, one for each index of `grp`. A program takes and returns all parts, laid end to end along the dimension named above; an argument that names none is the same for every part. Nothing has to cross between parts.
Inputs may be any that keep to these rules, and one draw needn't show every extreme that they name: `opt_lengths`: within each scoring group the 8 lengths sum to 320, and the longest option of each group has exactly 64 tokens in every draw.
All inputs are finite; a program needn't handle non-finite values.
Results may differ from a plain program's by a relative error of at most 0.017.
Values may be sent and summed in bfloat16 or wider, within the bound.
A program may use at most 64 MiB of HBM per device.

v0:
```python
import jax
import jax.numpy as jnp
from jax import lax
from jax.sharding import PartitionSpec as P

DH = 128
norm_epsilon = 1e-05


def entering(value, axis, join, neutral):
    place = lax.axis_index(axis)
    gathered = lax.all_gather(value.astype(jnp.bfloat16), axis)
    state = jnp.zeros_like(value) + jnp.asarray(neutral, value.dtype)

    def one(hop, state):
        return join(state, lax.dynamic_index_in_dim(gathered, hop, 0, False).astype(value.dtype))

    return lax.fori_loop(0, place, one, state)


def head_norm(attended, gain, mask):
    mean_square = jnp.mean(attended * attended, axis=-1, keepdims=True)
    return (attended * lax.rsqrt(mean_square + norm_epsilon) * gain * mask).astype(jnp.bfloat16)


def combine_sum(earlier, later):
    return earlier + later


def grouped_project(rows, weight_columns, groups):
    count = rows.shape[0]
    flat = rows.reshape(count, groups, rows.shape[1] // groups)
    weight_groups = weight_columns.reshape(
        groups, weight_columns.shape[0] // groups, weight_columns.shape[1]
    )
    partial_value = jnp.einsum(
        "rgk,gkd->grd", flat, weight_groups, preferred_element_type=jnp.float32
    )
    partial_value = lax.optimization_barrier(partial_value.astype(jnp.bfloat16)).astype(jnp.float32)
    return jnp.sum(partial_value, axis=0).astype(jnp.bfloat16)


def on_device(
    queries,
    keys,
    values,
    opt_queries,
    opt_keys,
    opt_values,
    opt_offsets,
    opt_lengths,
    norm_gain,
    out_weight,
):
    highest = lax.Precision.HIGHEST
    tok_rows = queries.shape[0]
    heads = queries.shape[1] // DH
    opt_count = opt_queries.shape[0]
    slot_count = opt_queries.shape[1]
    group_count = lax.axis_size(("head", "sub"))
    weight_columns = lax.all_to_all(
        out_weight, ("head", "sub"), split_axis=1, concat_axis=0, tiled=True
    )
    block_q = queries.reshape(tok_rows, heads, DH)
    block_k = keys.reshape(tok_rows, heads, DH)
    block_v = values.reshape(tok_rows, heads, DH)
    gain = norm_gain.reshape(heads, DH)
    states = jnp.einsum("thd,the->hde", block_k, block_v, precision=highest)
    positions = jnp.arange(tok_rows, dtype=jnp.int32)
    causal = (positions[:, None] >= positions[None, :]).astype(jnp.float32)
    scores = jnp.einsum("thd,shd->hts", block_q, block_k, precision=highest) * causal[None]
    intra = jnp.einsum("hts,she->the", scores, block_v, precision=highest)
    opt_q = opt_queries.reshape(opt_count, slot_count, heads, DH)
    opt_k = opt_keys.reshape(opt_count, slot_count, heads, DH)
    opt_v = opt_values.reshape(opt_count, slot_count, heads, DH)
    before = (positions[None, :] < opt_offsets[:, None]).astype(jnp.float32)
    local = jnp.einsum("ot,thd,the->ohde", before, block_k, block_v, precision=highest)
    slots = jnp.arange(slot_count, dtype=jnp.int32)
    slot_causal = (slots[:, None] >= slots[None, :]).astype(jnp.float32)
    opt_scores = (
        jnp.einsum("oihd,ojhd->ohij", opt_q, opt_k, precision=highest) * slot_causal[None, None]
    )
    opt_intra = jnp.einsum("ohij,ojhe->oihe", opt_scores, opt_v, precision=highest)
    prefix = entering(states, "seq", combine_sum, jnp.zeros_like(states))
    inter = jnp.einsum("thd,hde->the", block_q, prefix, precision=highest)
    context_normed = head_norm(inter + intra, gain, 1.0).reshape(tok_rows, heads * DH)
    opt_state = prefix[None] + local
    opt_inter = jnp.einsum("oihd,ohde->oihe", opt_q, opt_state, precision=highest)
    valid = (slots[None, :] < opt_lengths[:, None]).astype(jnp.float32)
    opt_normed = head_norm(opt_inter + opt_intra, gain, valid[:, :, None, None]).reshape(
        opt_count * slot_count, heads * DH
    )
    gathered_ctx, gathered_opt = (
        lax.all_gather(context_normed, ("head", "sub"), axis=1, tiled=True),
        lax.all_gather(opt_normed, ("head", "sub"), axis=1, tiled=True),
    )
    context_out = grouped_project(gathered_ctx, weight_columns, group_count)
    opt_rows = grouped_project(gathered_opt, weight_columns, group_count)
    option_out = opt_rows.reshape(opt_count, slot_count, opt_rows.shape[1])
    return (context_out, option_out)


def solution(mesh):
    placed = (
        P(("grp", "seq"), ("head", "sub")),
        P(("grp", "seq"), ("head", "sub")),
        P(("grp", "seq"), ("head", "sub")),
        P(("grp", "seq"), None, ("head", "sub")),
        P(("grp", "seq"), None, ("head", "sub")),
        P(("grp", "seq"), None, ("head", "sub")),
        P(("grp", "seq")),
        P(("grp", "seq")),
        P(("head", "sub")),
        P(("head", "sub"), None),
    )
    return jax.shard_map(
        on_device,
        mesh=mesh,
        in_specs=placed,
        out_specs=(P(("grp", "seq"), ("head", "sub")), P(("grp", "seq"), None, ("head", "sub"))),
        check_vma=False,
    )
```

profile of v0, /device:TPU:0, one launch (start us, length us, event | category | flops | bytes accessed | tf_op | source)
XLA Modules:
  0.0 91.5 jit_solution(10964770409362976219)
XLA Ops:
  0.6 0.0 copy-start
  0.6 6.5 %copy.40 = bf16[512,4096]{0,1:T(8,128)(2,1)} copy(bf16[512,4096]{1,0:T(8,128)(2,1)} %param.21) | data formatting | bytes 8388608 | tf_op args[9]
  7.2 6.3 %copy.41 = bf16[512,4,1024]{2,0,1:T(8,128)(2,1)} copy(bf16[512,4,1024]{0,2,1:T(8,128)(2,1)} %bitcast.132) | data formatting | bytes 8388608 | tf_op jit(solution)/shard_map/all_to_all | solution.py:61
  13.5 0.0 copy-start.1
  13.5 5.0 %all-to-all-start = ((bf16[512,4,1024]{2,0,1:T(8,128)(2,1)}), bf16[512,4,1024]{2,0,1:T(8,128)(2,1)}, u32[]{:S(2)}, u32[]{:S(2)}) async-start(bf16[512,4,1024]{2,0,1:T(8,128)(2,1)} %copy.41), calls=%async_computation | async-start | bytes 8388608 | tf_op jit(solution)/shard_map/all_to_all | solution.py:61
  18.5 0.0 copy-start.8
  18.5 0.0 copy-start.4
  18.5 0.0 copy-start.5
  18.5 0.0 copy-start.9
  18.6 0.0 copy-done
  18.6 0.0 copy-done.1
  18.6 0.0 copy-start.6
  18.6 1.1 %convolution_convert_fusion = bf16[4,128,128]{2,1,0:T(8,128)(2,1)S(1)} fusion(f32[192,512]{1,0:T(8,128)S(1)} %copy-done.1, f32[192,512]{1,0:T(8,128)S(1)} %copy-done), kind=kOutput, calls=%fused_computation.17 | convolution fusion | flops 151060480 | bytes 917504 | tf_op jit(solution)/shard_map/thd,the->hde/dot_general | solution.py:68
  19.7 17.9 %all-gather = bf16[16,128,128]{2,1,0:T(8,128)(2,1)S(1)} all-gather(bf16[4,128,128]{2,1,0:T(8,128)(2,1)S(1)} %convolution_convert_fusion), channel_id=2, replica_groups=mesh['grp'=2,'seq'=4,'head'=2,'sub'=2] {'seq'}, dimensions={0}, use_global_device_ids=true | all-gather | bytes 655360 | tf_op jit(solution)/shard_map/all_gather | solution.py:12
  37.6 0.0 copy-start.7
  37.6 0.0 copy-done.8
  37.6 0.0 copy-start.3
  37.6 0.1 fusion.39
  37.7 0.0 copy-done.4
  37.7 0.0 copy-done.5
  37.7 0.5 convolution_multiply_fusion.1
  38.3 0.0 copy-done.9
  38.3 0.1 compare_convert_fusion.1
  38.4 1.9 %fusion.10 = f32[2,4,128,128]{3,2,1,0:T(8,128)S(1)} fusion(f32[192,4,128]{2,0,1:T(8,128)S(1)} %copy_bitcast_fusion, f32[192,2]{0,1:T(2,128)S(1)} %fusion.39, f32[4,128,128]{2,1,0:T(8,128)S(1)} %get-tuple-element.25, f32[192,512]{1,0:T(8,128)S(1)} %copy-done.1), kind=kOutput, calls=%fused_computation.9 | convolution fusion | flops 302317568 | bytes 1574400 | tf_op jit(solution)/shard_map/ot,thd,the->ohde/dot_general | solution.py:77
  40.3 0.6 convolution_bitcast_fusion.3
  40.9 0.0 copy-done.6
  40.9 0.5 multiply_reduce_fusion.1
  41.4 0.0 copy-done.7
  41.4 0.2 multiply_convert_fusion.1
  41.6 0.1 copy.49
  41.7 29.2 %all_gather.15 = bf16[128,2048]{1,0:T(8,128)(2,1)S(1)} all-gather(bf16[128,512]{1,0:T(8,128)(2,1)S(1)} %bitcast.136), channel_id=1, replica_groups=mesh['grp'=2,'seq'=4,'head'=2,'sub'=2] {'head','sub'}, dimensions={1}, use_global_device_ids=true | all-gather | bytes 655360 | tf_op jit(solution)/shard_map/all_gather | solution.py:95
  70.9 1.0 %copy.50 = bf16[128,2048]{0,1:T(8,128)(2,1)} copy(bf16[128,2048]{1,0:T(8,128)(2,1)S(1)} %all_gather.15) | data formatting | bytes 1048576 | tf_op jit(solution)/shard_map/all_gather | solution.py:95
  72.0 0.0 copy-done.3
  72.0 0.5 convolution_bitcast_fusion.1
  72.5 0.8 convolution_multiply_fusion
  73.3 1.0 %multiply_reduce_fusion = (f32[192,4]{0,1:T(4,128)S(1)}, f32[192,4,128]{2,0,1:T(8,128)S(1)}) fusion(f32[192,4,128]{2,0,1:T(8,128)S(1)} %convolution_bitcast_fusion.1, f32[4,192,192]{2,1,0:T(8,128)S(1)} %convolution_multiply_fusion, f32[192,512]{1,0:T(8,128)S(1)} %copy-done.1), kind=kOutput, calls=%fused_computation.31 | convolution fusion | flops 226786560 | bytes 1772544 | tf_op jit(solution)/shard_map/hts,she->the/dot_general | solution.py:72
  74.3 0.2 copy_bitcast_fusion.1
  74.5 8.7 %all_gather.14 = bf16[192,2048]{1,0:T(8,128)(2,1)S(1)} all-gather(bf16[192,512]{1,0:T(8,128)(2,1)S(1)} %copy_bitcast_fusion.1), channel_id=1, replica_groups=mesh['grp'=2,'seq'=4,'head'=2,'sub'=2] {'head','sub'}, dimensions={1}, use_global_device_ids=true | all-gather | bytes 983040 | tf_op jit(solution)/shard_map/all_gather | solution.py:94
  83.2 0.0 all-to-all-done
  83.2 0.0 copy-start.2
  83.2 3.2 %fusion.4 = bf16[4,192,1024]{2,1,0:T(8,128)(2,1)S(1)} fusion(bf16[512,4,1024]{2,0,1:T(8,128)(2,1)} %all-to-all-done, bf16[24,4,8,512]{3,2,1,0:T(8,128)(2,1)S(1)} %bitcast.133), kind=kOutput, calls=%fused_computation.5 | convolution fusion | flops 806092800 | bytes 6553600 | tf_op jit(solution)/shard_map/rgk,gkd->grd/dot_general | solution.py:36
  86.4 0.0 copy-done.2
  86.4 3.0 %fusion.7 = bf16[4,128,1024]{2,1,0:T(8,128)(2,1)S(1)} fusion(bf16[128,4,512]{0,2,1:T(8,128)(2,1)S(1)} %bitcast.134, bf16[512,4,1024]{2,0,1:T(8,128)(2,1)} %all-to-all-done), kind=kOutput, calls=%fused_computation.6 | convolution fusion | flops 537395200 | bytes 5767168 | tf_op jit(solution)/shard_map/rgk,gkd->grd/dot_general | solution.py:36
  89.4 1.1 %reduce_sum.43 = bf16[192,1024]{1,0:T(8,128)(2,1)} reduce(bf16[4,192,1024]{2,1,0:T(8,128)(2,1)S(1)} %fusion.4, bf16[]{:T(256)} %constant.28.clone.1), dimensions={0}, to_apply=%region_3.4 | reduce | flops 589824 | bytes 1966082 | tf_op jit(solution)/shard_map/reduce_sum | solution.py:40
  90.6 0.9 %reduce_sum.45 = bf16[128,1024]{1,0:T(8,128)(2,1)} reduce(bf16[4,128,1024]{2,1,0:T(8,128)(2,1)S(1)} %fusion.7, bf16[]{:T(256)} %constant.28.clone.1), dimensions={0}, to_apply=%region_5.6 | reduce | flops 393216 | bytes 1310722 | tf_op jit(solution)/shard_map/reduce_sum | solution.py:40
  (8 shorter events, 0.1 us)
Async XLA Ops:
  0.6 17.9 %copy-start = (f32[192,512]{1,0:T(8,128)S(1)}, f32[192,512]{1,0:T(8,128)}, u32[]{:S(2)}) copy-start(f32[192,512]{1,0:T(8,128)} %param.13) | copy-start | bytes 1179652
  13.5 5.1 %copy-start.1 = (f32[192,512]{1,0:T(8,128)S(1)}, f32[192,512]{1,0:T(8,128)}, u32[]{:S(2)}) copy-start(f32[192,512]{1,0:T(8,128)} %param.14) | copy-start | bytes 1179652
  13.5 69.7 %all-to-all-start = ((bf16[512,4,1024]{2,0,1:T(8,128)(2,1)}), bf16[512,4,1024]{2,0,1:T(8,128)(2,1)}, u32[]{:S(2)}, u32[]{:S(2)}) async-start(bf16[512,4,1024]{2,0,1:T(8,128)(2,1)} %copy.41), calls=%async_computation | async-start | bytes 8388608 | tf_op jit(solution)/shard_map/all_to_all | solution.py:61
  18.5 19.1 %copy-start.8 = (s32[2]{0:T(128)S(1)}, s32[2]{0:T(128)}, u32[]{:S(2)}) copy-start(s32[2]{0:T(128)} %param.18) | copy-start | bytes 28
  18.5 19.2 %copy-start.4 = (f32[2,64,512]{2,1,0:T(8,128)S(1)}, f32[2,64,512]{2,1,0:T(8,128)}, u32[]{:S(2)}) copy-start(f32[2,64,512]{2,1,0:T(8,128)} %param.15) | copy-start | bytes 786436
  18.5 19.2 %copy-start.5 = (f32[2,64,512]{2,1,0:T(8,128)S(1)}, f32[2,64,512]{2,1,0:T(8,128)}, u32[]{:S(2)}) copy-start(f32[2,64,512]{2,1,0:T(8,128)} %param.16) | copy-start | bytes 786436
  18.5 19.8 %copy-start.9 = (s32[2]{0:T(128)S(1)}, s32[2]{0:T(128)}, u32[]{:S(2)}) copy-start(s32[2]{0:T(128)} %param.19) | copy-start | bytes 28
  18.6 22.2 %copy-start.6 = (f32[2,64,512]{2,1,0:T(8,128)S(1)}, f32[2,64,512]{2,1,0:T(8,128)}, u32[]{:S(2)}) copy-start(f32[2,64,512]{2,1,0:T(8,128)} %param.17) | copy-start | bytes 786436
  37.6 3.8 %copy-start.7 = (f32[512]{0:T(512)S(1)}, f32[512]{0:T(512)}, u32[]{:S(2)}) copy-start(f32[512]{0:T(512)} %param.20) | copy-start | bytes 6148
  37.6 34.4 %copy-start.3 = (f32[192,512]{1,0:T(8,128)S(1)}, f32[192,512]{1,0:T(8,128)}, u32[]{:S(2)}) copy-start(f32[192,512]{1,0:T(8,128)} %param.12) | copy-start | bytes 1179652
  83.2 3.2 %copy-start.2 = (bf16[128,2048]{0,1:T(8,128)(2,1)S(1)}, bf16[128,2048]{0,1:T(8,128)(2,1)}, u32[]{:S(2)}) copy-start(bf16[128,2048]{0,1:T(8,128)(2,1)} %copy.50) | copy-start | bytes 1572868
where the time goes:
time: 92 us; the launch traced here: 91.5 us
  blocking collectives  55.8 us (61%)
  local copies, waits for them, and re-layouts  14.1 us (15%)
  matrix products  13.1 us (14%)
  starting transfers between devices  4.97 us (5%)
  other arithmetic  2.58 us (3%)
    all_gather x1, blocking collectives, on_device(): lax.all_gather(opt_normed, ('head', 'sub'), axis=1, tiled=True)  29.2 us
    all_gather x1, blocking collectives, entering(): gathered = lax.all_gather(value.astype(jnp.bfloat16), axis)  17.9 us
    all_gather x1, blocking collectives, on_device(): lax.all_gather(context_normed, ('head', 'sub'), axis=1, tiled=True)  8.71 us
    unnamed x22, local copies, waits for them, and re-layouts  6.62 us
    all_to_all x1, local copies, waits for them, and re-layouts, on_device(): lax.all_to_all(out_weight, ('head', 'sub'), split_axis=1, concat_axis=0,...  6.33 us
    dot_general x2, matrix products, grouped_project(): jnp.einsum('rgk,gkd->grd', flat, weight_groups, preferred_element_type=jn...  6.22 us
    all_to_all x1, starting transfers between devices, on_device(): lax.all_to_all(out_weight, ('head', 'sub'), split_axis=1, concat_axis=0,...  4.97 us
    reduce_sum x2, other arithmetic, grouped_project(): return jnp.sum(partial_value, axis=0).astype(jnp.bfloat16)  2.06 us
  transfers between devices with their start and end apart: 1, of which 0 were waited for; matrix products, arithmetic and copies ran while one was open for 9% of the time, Pallas kernels for 0%

commit v1 on v0

--- a/solution.py
+++ b/solution.py
@@ -5,6 +5,15 @@
 
 DH = 128
 norm_epsilon = 1e-05
+settle_local_data_on = lambda u_in: jnp.concatenate(
+    lax.all_to_all(
+        jnp.stack(jnp.split(u_in, lax.axis_size(("head", "sub")), axis=1)),
+        split_axis=0,
+        concat_axis=0,
+        axis_name=("head", "sub"),
+    ),
+    axis=0,
+)
 
 
 def entering(value, axis, join, neutral):
@@ -58,9 +67,7 @@
     opt_count = opt_queries.shape[0]
     slot_count = opt_queries.shape[1]
     group_count = lax.axis_size(("head", "sub"))
-    weight_columns = lax.all_to_all(
-        out_weight, ("head", "sub"), split_axis=1, concat_axis=0, tiled=True
-    )
+    weight_columns = settle_local_data_on(out_weight)
     block_q = queries.reshape(tok_rows, heads, DH)
     block_k = keys.reshape(tok_rows, heads, DH)
     block_v = values.reshape(tok_rows, heads, DH)

time: 92 us -> 83.5 us (0.908)
  local copies, waits for them, and re-layouts: 14.1 us -> 3.18 us
  other arithmetic: 2.58 us -> 4.85 us
    unnamed x22 -> x21, local copies, waits for them, and re-layouts: 6.62 us -> 0.08 us
    all_to_all x1 -> x0, local copies, waits for them, and re-layouts: 6.33 us -> none  [on_device(): lax.all_to_all(out_weight, ('head', 'sub'), split_axis=1, concat_axis=0,...]
    another operation x0 -> x1, local copies, waits for them, and re-layouts: none -> 2.68 us  [jnp.stack(jnp.split(u_in, lax.axis_size(('head', 'sub')), axis=1))]
    another operation x1 -> x2, other arithmetic: 0.07 us -> 2.34 us  [the longest x1 2.27 us: jnp.stack(jnp.split(u_in, lax.axis_size(('head', 'sub')), axis=1))]
where the time goes in v1:
time: 83.5 us; the launch traced here: 83.3 us
  blocking collectives  56.3 us (67%)
  matrix products  13.1 us (16%)
  starting transfers between devices  4.96 us (6%)
  other arithmetic  4.85 us (6%)
  local copies, waits for them, and re-layouts  3.18 us (4%)
  between operations  0.91 us (1%)
    all_gather x1, blocking collectives, on_device(): lax.all_gather(opt_normed, ('head', 'sub'), axis=1, tiled=True)  29.2 us
    all_gather x1, blocking collectives, entering(): gathered = lax.all_gather(value.astype(jnp.bfloat16), axis)  17.9 us
    all_gather x1, blocking collectives, on_device(): lax.all_gather(context_normed, ('head', 'sub'), axis=1, tiled=True)  9.16 us
    dot_general x2, matrix products, grouped_project(): jnp.einsum('rgk,gkd->grd', flat, weight_groups, preferred_element_type=jn...  6.23 us
    all_to_all x1, starting transfers between devices, lax.all_to_all(jnp.stack(jnp.split(u_in, lax.axis_size(('head', 'sub')),...  4.96 us
    another operation x1, local copies, waits for them, and re-layouts, jnp.stack(jnp.split(u_in, lax.axis_size(('head', 'sub')), axis=1))  2.68 us
    another operation x1, other arithmetic, jnp.stack(jnp.split(u_in, lax.axis_size(('head', 'sub')), axis=1))  2.27 us
    reduce_sum x2, other arithmetic, grouped_project(): return jnp.sum(partial_value, axis=0).astype(jnp.bfloat16)  2.06 us
  transfers between devices with their start and end apart: 1, of which 0 were waited for; matrix products, arithmetic and copies ran while one was open for 9% of the time, Pallas kernels for 0%

profile of v1, /device:TPU:0, one launch (start us, length us, event | category | flops | bytes accessed | tf_op | source)
XLA Modules:
  0.0 83.3 jit_solution(1832997538982441359)
XLA Ops:
  0.6 0.0 copy-start
  0.6 2.7 %slice_bitcast_fusion.3 = (bf16[1,512,1024]{2,1,0:T(8,128)(2,1)S(1)}, bf16[1,512,1024]{2,1,0:T(8,128)(2,1)S(1)}, bf16[1,512,1024]{2,1,0:T(8,128)(2,1)S(1)}, bf16[1,512,1024]{2,1,0:T(8,128)(2,1)S(1)}) fusion(bf16[512,4096]{1,0:T(8,128)(2,1)} %param.21), kind=kLoop, calls=%fused_computation.18 | loop fusion | bytes 8388608 | tf_op jit(solution)/shard_map/stack | solution.py:10
  3.3 2.3 %pad_maximum_fusion = bf16[4,512,1024]{2,1,0:T(8,128)(2,1)} fusion(bf16[1,512,1024]{2,1,0:T(8,128)(2,1)S(1)} %get-tuple-element.36, bf16[1,512,1024]{2,1,0:T(8,128)(2,1)S(1)} %get-tuple-element.37, bf16[1,512,1024]{2,1,0:T(8,128)(2,1)S(1)} %get-tuple-element.35, bf16[1,512,1024]{2,1,0:T(8,128)(2,1)S(1)} %get-tuple-element.34), kind=kLoop, calls=%fused_computation.1 | loop fusion | flops 6291456 | bytes 8388608 | tf_op jit(solution)/shard_map/stack | solution.py:10
  5.6 0.0 copy-start.2
  5.6 5.0 %all-to-all-start = ((bf16[4,512,1024]{2,1,0:T(8,128)(2,1)}), bf16[4,512,1024]{2,1,0:T(8,128)(2,1)}, u32[]{:S(2)}, u32[]{:S(2)}) async-start(bf16[4,512,1024]{2,1,0:T(8,128)(2,1)} %pad_maximum_fusion), calls=%async_computation | async-start | bytes 8388608 | tf_op jit(solution)/shard_map/all_to_all | solution.py:9
  10.6 0.0 copy-start.8
  10.6 0.0 copy-start.4
  10.6 0.0 copy-start.5
  10.6 0.0 copy-start.9
  10.6 0.0 copy-done
  10.7 0.0 copy-done.2
  10.7 0.0 copy-start.6
  10.7 1.1 %convolution_convert_fusion.2 = bf16[4,128,128]{2,1,0:T(8,128)(2,1)S(1)} fusion(f32[192,512]{1,0:T(8,128)S(1)} %copy-done.2, f32[192,512]{1,0:T(8,128)S(1)} %copy-done), kind=kOutput, calls=%fused_computation.14 | convolution fusion | flops 151060480 | bytes 917504 | tf_op jit(solution)/shard_map/thd,the->hde/dot_general | solution.py:75
  11.8 17.9 %all-gather = bf16[16,128,128]{2,1,0:T(8,128)(2,1)S(1)} all-gather(bf16[4,128,128]{2,1,0:T(8,128)(2,1)S(1)} %convolution_convert_fusion.2), channel_id=2, replica_groups=mesh['grp'=2,'seq'=4,'head'=2,'sub'=2] {'seq'}, dimensions={0}, use_global_device_ids=true | all-gather | bytes 655360 | tf_op jit(solution)/shard_map/all_gather | solution.py:21
  29.7 0.0 copy-start.7
  29.7 0.0 copy-done.8
  29.7 0.0 copy-start.3
  29.7 0.1 fusion.29
  29.8 0.0 copy-done.4
  29.8 0.0 copy-done.5
  29.8 0.5 convolution_multiply_fusion.1
  30.3 0.0 copy-done.9
  30.4 0.1 compare_convert_fusion.1
  30.4 1.9 %fusion = f32[2,4,128,128]{3,2,1,0:T(8,128)S(1)} fusion(f32[192,4,128]{2,0,1:T(8,128)S(1)} %copy_bitcast_fusion, f32[192,2]{0,1:T(2,128)S(1)} %fusion.29, f32[4,128,128]{2,1,0:T(8,128)S(1)} %get-tuple-element.25, f32[192,512]{1,0:T(8,128)S(1)} %copy-done.2), kind=kOutput, calls=%fused_computation.6 | convolution fusion | flops 302317568 | bytes 1574400 | tf_op jit(solution)/shard_map/ot,thd,the->ohde/dot_general | solution.py:84
  32.4 0.6 convolution_bitcast_fusion.3
  32.9 0.0 copy-done.6
  32.9 0.5 multiply_reduce_fusion.1
  33.5 0.0 copy-done.7
  33.5 0.2 multiply_convert_fusion.1
  33.6 0.1 copy.45
  33.8 29.2 %all_gather.15 = bf16[128,2048]{1,0:T(8,128)(2,1)S(1)} all-gather(bf16[128,512]{1,0:T(8,128)(2,1)S(1)} %bitcast.135), channel_id=1, replica_groups=mesh['grp'=2,'seq'=4,'head'=2,'sub'=2] {'head','sub'}, dimensions={1}, use_global_device_ids=true | all-gather | bytes 655360 | tf_op jit(solution)/shard_map/all_gather | solution.py:102
  63.0 0.3 copy.46
  63.3 0.0 copy-done.3
  63.3 0.5 convolution_bitcast_fusion.1
  63.8 0.8 convolution_multiply_fusion
  64.6 1.0 %multiply_reduce_fusion = (f32[192,4]{0,1:T(4,128)S(1)}, f32[192,4,128]{2,0,1:T(8,128)S(1)}) fusion(f32[192,4,128]{2,0,1:T(8,128)S(1)} %convolution_bitcast_fusion.1, f32[4,192,192]{2,1,0:T(8,128)S(1)} %convolution_multiply_fusion, f32[192,512]{1,0:T(8,128)S(1)} %copy-done.2), kind=kOutput, calls=%fused_computation.32 | convolution fusion | flops 226786560 | bytes 1772544 | tf_op jit(solution)/shard_map/hts,she->the/dot_general | solution.py:79
  65.6 0.2 copy_bitcast_fusion.1
  65.8 9.2 %all_gather.14 = bf16[192,2048]{1,0:T(8,128)(2,1)} all-gather(bf16[192,512]{1,0:T(8,128)(2,1)S(1)} %copy_bitcast_fusion.1), channel_id=1, replica_groups=mesh['grp'=2,'seq'=4,'head'=2,'sub'=2] {'head','sub'}, dimensions={1}, use_global_device_ids=true | all-gather | bytes 983040 | tf_op jit(solution)/shard_map/all_gather | solution.py:101
  75.0 0.0 all-to-all-done
  75.0 0.0 copy-start.1
  75.0 3.0 %convolution_convert_fusion.1 = bf16[4,128,1024]{2,1,0:T(8,128)(2,1)S(1)} fusion(bf16[128,4,512]{0,2,1:T(8,128)(2,1)S(1)} %bitcast.133, bf16[4,512,1024]{2,1,0:T(8,128)(2,1)} %all-to-all-done), kind=kOutput, calls=%fused_computation.3 | convolution fusion | flops 537395200 | bytes 5767168 | tf_op jit(solution)/shard_map/rgk,gkd->grd/dot_general | solution.py:45
  78.0 0.0 copy-done.1
  78.0 3.2 %convolution_convert_fusion = bf16[4,192,1024]{2,1,0:T(8,128)(2,1)S(1)} fusion(bf16[4,512,1024]{2,1,0:T(8,128)(2,1)} %all-to-all-done, bf16[24,4,8,512]{3,2,1,0:T(8,128)(2,1)S(1)} %bitcast.132), kind=kOutput, calls=%fused_computation.2 | convolution fusion | flops 806092800 | bytes 6553600 | tf_op jit(solution)/shard_map/rgk,gkd->grd/dot_general | solution.py:45
  81.2 0.9 %reduce_sum.45 = bf16[128,1024]{1,0:T(8,128)(2,1)} reduce(bf16[4,128,1024]{2,1,0:T(8,128)(2,1)S(1)} %convolution_convert_fusion.1, bf16[]{:T(256)} %constant.28.clone.1), dimensions={0}, to_apply=%region_5.6 | reduce | flops 393216 | bytes 1310722 | tf_op jit(solution)/shard_map/reduce_sum | solution.py:49
  82.2 1.1 %reduce_sum.43 = bf16[192,1024]{1,0:T(8,128)(2,1)} reduce(bf16[4,192,1024]{2,1,0:T(8,128)(2,1)S(1)} %convolution_convert_fusion, bf16[]{:T(256)} %constant.28.clone.1), dimensions={0}, to_apply=%region_3.4 | reduce | flops 589824 | bytes 1966082 | tf_op jit(solution)/shard_map/reduce_sum | solution.py:49
  (8 shorter events, 0.1 us)
Async XLA Ops:
  0.6 10.0 %copy-start = (f32[192,512]{1,0:T(8,128)S(1)}, f32[192,512]{1,0:T(8,128)}, u32[]{:S(2)}) copy-start(f32[192,512]{1,0:T(8,128)} %param.13) | copy-start | bytes 1179652
  5.6 5.1 %copy-start.2 = (f32[192,512]{1,0:T(8,128)S(1)}, f32[192,512]{1,0:T(8,128)}, u32[]{:S(2)}) copy-start(f32[192,512]{1,0:T(8,128)} %param.14) | copy-start | bytes 1179652
  5.6 69.4 %all-to-all-start = ((bf16[4,512,1024]{2,1,0:T(8,128)(2,1)}), bf16[4,512,1024]{2,1,0:T(8,128)(2,1)}, u32[]{:S(2)}, u32[]{:S(2)}) async-start(bf16[4,512,1024]{2,1,0:T(8,128)(2,1)} %pad_maximum_fusion), calls=%async_computation | async-start | bytes 8388608 | tf_op jit(solution)/shard_map/all_to_all | solution.py:9
  10.6 19.1 %copy-start.8 = (s32[2]{0:T(128)S(1)}, s32[2]{0:T(128)}, u32[]{:S(2)}) copy-start(s32[2]{0:T(128)} %param.18) | copy-start | bytes 28
  10.6 19.2 %copy-start.4 = (f32[2,64,512]{2,1,0:T(8,128)S(1)}, f32[2,64,512]{2,1,0:T(8,128)}, u32[]{:S(2)}) copy-start(f32[2,64,512]{2,1,0:T(8,128)} %param.15) | copy-start | bytes 786436
  10.6 19.2 %copy-start.5 = (f32[2,64,512]{2,1,0:T(8,128)S(1)}, f32[2,64,512]{2,1,0:T(8,128)}, u32[]{:S(2)}) copy-start(f32[2,64,512]{2,1,0:T(8,128)} %param.16) | copy-start | bytes 786436
  10.6 19.7 %copy-start.9 = (s32[2]{0:T(128)S(1)}, s32[2]{0:T(128)}, u32[]{:S(2)}) copy-start(s32[2]{0:T(128)} %param.19) | copy-start | bytes 28
  10.7 22.2 %copy-start.6 = (f32[2,64,512]{2,1,0:T(8,128)S(1)}, f32[2,64,512]{2,1,0:T(8,128)}, u32[]{:S(2)}) copy-start(f32[2,64,512]{2,1,0:T(8,128)} %param.17) | copy-start | bytes 786436
  29.7 3.8 %copy-start.7 = (f32[512]{0:T(512)S(1)}, f32[512]{0:T(512)}, u32[]{:S(2)}) copy-start(f32[512]{0:T(512)} %param.20) | copy-start | bytes 6148
  29.7 33.6 %copy-start.3 = (f32[192,512]{1,0:T(8,128)S(1)}, f32[192,512]{1,0:T(8,128)}, u32[]{:S(2)}) copy-start(f32[192,512]{1,0:T(8,128)} %param.12) | copy-start | bytes 1179652
  75.0 3.0 %copy-start.1 = (bf16[192,2048]{1,0:T(8,128)(2,1)S(1)}, bf16[192,2048]{1,0:T(8,128)(2,1)}, u32[]{:S(2)}) copy-start(bf16[192,2048]{1,0:T(8,128)(2,1)} %all_gather.14) | copy-start | bytes 2359300
